TPU v7x, 32 devices: a whole 2x2x4 slice. The times are simulated.
32 devices in a mesh: groups: 2 (over x), tm: 16 (over z, y, core).
Axes of the slice: x: 2, y: 2, z: 4, core: 2. Of those that a mesh axis runs over, the one named last changes fastest.
Arguments:
- points: float32 [32, 64, 2048], P(('groups', 'tm')), parts along dimension 0, may hold values from -4 to 4
- potentials: float32 [32, 224, 2048], P(('groups', 'tm')), parts along dimension 0, may hold values from 0.5 to 25, as said below
- supports: int32 [32], P(('groups', 'tm')), parts along dimension 0, may hold values from 512 to 2048, as said below
Outputs:
- messages: float32 [32, 224, 2048], P(('groups', 'tm')), parts along dimension 0
- log_scale: float32 [448], P('groups'), parts along dimension 0
There are 2 independent parts, one for each index of `groups`. A program takes and returns all parts, laid end to end along the dimension named above; each array names one. Nothing has to cross between parts.
Inputs may be any that keep to these rules, and one draw needn't show every extreme that they name: `supports`: the first and the last time slice have all 2048 points live; every other slice has between 512 and 1024 live points, at its first positions. `potentials`: positive scalings.
All inputs are finite; a program needn't handle non-finite values.
Results may differ from a plain program's by a relative error of at most 0.017.
Values may be sent and summed in bfloat16 or wider, within the bound.
No kernel may reach another device: no remote copies, remote signals or barrier semaphores. Data moves between devices by JAX's collectives and lax.ppermute only.
A program may use at most 64 MiB of HBM per device.

v0:
```python
import jax
import jax.numpy as jnp
from jax import lax
from jax.sharding import PartitionSpec as P

MICRO = 32
A_DECAY = 0.8
EPS_SCALE = 0.05


def shifted(value, axis, steps):
    count = lax.axis_size(axis)
    initial, last = (max(0, -steps), min(count, count - steps))
    return lax.ppermute(value, axis, [(source, source + steps) for source in range(initial, last)])


def slice_kernel(source, target):
    dim_count, point_count = source.shape
    block_rows = min(512, point_count)
    inv_width = 1.0 / (2.0 * EPS_SCALE * dim_count)
    target_sq = jnp.sum(target * target, axis=0)
    pieces = jnp.transpose(
        source.reshape(dim_count, point_count // block_rows, block_rows), (1, 0, 2)
    )

    def one_block(segment):
        products = lax.dot_general(
            segment,
            target,
            (((0,), (0,)), ((), ())),
            precision=lax.Precision.HIGHEST,
            preferred_element_type=jnp.float32,
        )
        segment_sq = jnp.sum(segment * segment, axis=0)
        distance = (
            target_sq[None, :] + A_DECAY * A_DECAY * segment_sq[:, None] - 2.0 * A_DECAY * products
        )
        return jnp.exp(-inv_width * distance).astype(jnp.bfloat16)

    return lax.map(one_block, pieces).reshape(point_count, point_count)


def push_forward(weighted, kernel, live_row):
    pushed = jnp.dot(weighted, kernel, preferred_element_type=jnp.float32) * live_row[None, :]
    return (pushed, jnp.sum(pushed, axis=1))


def per_device(points, potentials, supports):
    local_slices, dim_count, point_count = points.shape
    all_cols = potentials.shape[1]
    tm_count = lax.axis_size("tm")
    position = lax.axis_index("tm")
    live_mask = (jnp.arange(point_count, dtype=jnp.int32)[None, :] < supports[:, None]).astype(
        jnp.float32
    )
    counts = supports.astype(jnp.float32)
    arrived = shifted(points[local_slices - 1], "tm", 1)
    sources = jnp.concatenate([arrived[None], points[:-1]], axis=0)
    kernels = lax.map(lambda paired: slice_kernel(paired[0], paired[1]), (sources, points))
    block_cols = MICRO
    batches = all_cols // block_cols
    phase_count = tm_count + batches - 1
    is_first = position == 0

    def section(incoming, block_id):
        block_pot = lax.dynamic_slice_in_dim(potentials, block_id * block_cols, block_cols, 1)
        pushed, column_sum = push_forward(incoming, kernels[0], live_mask[0])
        safe_sum = jnp.where(is_first, 1.0, column_sum)
        start_msg = jnp.broadcast_to(live_mask[0][None, :], pushed.shape)
        message = jnp.where(is_first, start_msg, pushed * (counts[0] / safe_sum)[:, None])
        outputs = [message]
        log_terms = [jnp.where(is_first, 0.0, jnp.log(safe_sum / counts[0]))]
        outgoing = (message * block_pot[local_slices - 1]).astype(jnp.bfloat16)
        return (jnp.stack(outputs), jnp.stack(log_terms), outgoing)

    def advance(phase, state_in):
        incoming, messages, log_parts = state_in
        block_id = phase - position
        active = (block_id >= 0) & (block_id < batches)
        clipped = jnp.clip(block_id, 0, batches - 1)

        def compute(operands):
            stored, stored_logs = operands
            block_msgs, block_logs, outgoing = section(incoming, clipped)
            stored = lax.dynamic_update_slice_in_dim(stored, block_msgs, clipped * block_cols, 1)
            stored_logs = lax.dynamic_update_slice_in_dim(
                stored_logs, block_logs, clipped * block_cols, 1
            )
            return (stored, stored_logs, outgoing)

        def skipped(operands):
            stored, stored_logs = operands
            return (stored, stored_logs, jnp.zeros((block_cols, point_count), jnp.bfloat16))

        messages, log_parts, outgoing = lax.cond(active, compute, skipped, (messages, log_parts))
        received = shifted(outgoing, "tm", 1)
        return (received, messages, log_parts)

    initial = (
        jnp.zeros((block_cols, point_count), jnp.bfloat16),
        jnp.zeros((local_slices, all_cols, point_count), jnp.float32),
        jnp.zeros((local_slices, all_cols), jnp.float32),
    )
    unused, messages, log_parts = lax.fori_loop(0, phase_count, advance, initial)
    local_log = jnp.sum(log_parts, axis=0)
    log_scale = lax.psum(local_log, "tm") / (tm_count * local_slices - 1)
    return (messages, log_scale)


def solution(mesh):
    placed = (P(("groups", "tm"), None, None), P(("groups", "tm"), None, None), P(("groups", "tm")))
    return jax.shard_map(
        per_device,
        mesh=mesh,
        in_specs=placed,
        out_specs=(P(("groups", "tm"), None, None), P("groups")),
        check_vma=False,
    )
```

profile of v0, /device:TPU:0, one launch (start us, length us, event | category | flops | bytes accessed | tf_op | source)
XLA Modules:
  0.0 334.8 jit_solution(13703646366627489090)
XLA Ops:
  4.9 26.2 %while.35 = (s32[]{:T(128)}, bf16[4,512,2048]{2,1,0:T(8,128)(2,1)}, f32[2048]{0:T(1024)S(1)}, f32[4,64,512]{2,1,0:T(8,128)S(1)}, f32[64,2048]{1,0:T(8,128)}, /*index=5*/s32[]{:T(128)}) while((s32[]{:T(128)}, bf16[4,512,2048]{2,1,0:T(8,128)(2,1)}, f32[2048]{0:T(1024)S(1)}, f32[4,64,512]{2,1,0:T(8,128)S(1)}, f32[64,2048]{1,0:T(8,128)}, ...), condition=%wide.region_3.0_spmd, body=%wide.region_1.3_spmd.sunk | while | flops 810614784 | bytes 2901065 | solution.py:40
  4.9 6.5 %fusion.26 = bf16[4,512,2048]{2,1,0:T(8,128)(2,1)} fusion(bf16[4,512,2048]{2,1,0:T(8,128)(2,1)} %get-tuple-element.449, s32[]{:T(128)} %get-tuple-element.448, f32[64,2048]{1,0:T(8,128)} %get-tuple-element.458, f32[512]{0:T(512)S(1)} %broadcast_multiply_fusion.3, f32[2048]{0:T(1024)S(1)} %get-tuple-element.456, f32[4,64,512]{2,1,0:T(8,128)S(1)} %get-tuple-element.457), kind=kOutput, calls=%fused_computation.3.clone.1 | convolution fusion | flops 810549248 | bytes 2763776 | tf_op jit(solution)/shard_map/while/body/eval_jaxpr/while/body/eval_jaxpr/dot_general | solution.py:27
  11.5 6.5 %fusion.26 = bf16[4,512,2048]{2,1,0:T(8,128)(2,1)} fusion(bf16[4,512,2048]{2,1,0:T(8,128)(2,1)} %get-tuple-element.449, s32[]{:T(128)} %get-tuple-element.448, f32[64,2048]{1,0:T(8,128)} %get-tuple-element.458, f32[512]{0:T(512)S(1)} %broadcast_multiply_fusion.3, f32[2048]{0:T(1024)S(1)} %get-tuple-element.456, f32[4,64,512]{2,1,0:T(8,128)S(1)} %get-tuple-element.457), kind=kOutput, calls=%fused_computation.3.clone.1 | convolution fusion | flops 810549248 | bytes 2763776 | tf_op jit(solution)/shard_map/while/body/eval_jaxpr/while/body/eval_jaxpr/dot_general | solution.py:27
  18.1 6.5 %fusion.26 = bf16[4,512,2048]{2,1,0:T(8,128)(2,1)} fusion(bf16[4,512,2048]{2,1,0:T(8,128)(2,1)} %get-tuple-element.449, s32[]{:T(128)} %get-tuple-element.448, f32[64,2048]{1,0:T(8,128)} %get-tuple-element.458, f32[512]{0:T(512)S(1)} %broadcast_multiply_fusion.3, f32[2048]{0:T(1024)S(1)} %get-tuple-element.456, f32[4,64,512]{2,1,0:T(8,128)S(1)} %get-tuple-element.457), kind=kOutput, calls=%fused_computation.3.clone.1 | convolution fusion | flops 810549248 | bytes 2763776 | tf_op jit(solution)/shard_map/while/body/eval_jaxpr/while/body/eval_jaxpr/dot_general | solution.py:27
  24.6 6.5 %fusion.26 = bf16[4,512,2048]{2,1,0:T(8,128)(2,1)} fusion(bf16[4,512,2048]{2,1,0:T(8,128)(2,1)} %get-tuple-element.449, s32[]{:T(128)} %get-tuple-element.448, f32[64,2048]{1,0:T(8,128)} %get-tuple-element.458, f32[512]{0:T(512)S(1)} %broadcast_multiply_fusion.3, f32[2048]{0:T(1024)S(1)} %get-tuple-element.456, f32[4,64,512]{2,1,0:T(8,128)S(1)} %get-tuple-element.457), kind=kOutput, calls=%fused_computation.3.clone.1 | convolution fusion | flops 810549248 | bytes 2763776 | tf_op jit(solution)/shard_map/while/body/eval_jaxpr/while/body/eval_jaxpr/dot_general | solution.py:27
  31.4 226.2 %while.36 = (s32[]{:T(128)}, bf16[32,2048]{1,0:T(8,128)(2,1)S(1)}, f32[1,224,2048]{2,1,0:T(8,128)S(1)}, f32[1,224]{1,0:T(1,128)S(1)}, s32[]{:T(128)}, /*index=5*...) while((s32[]{:T(128)}, bf16[32,2048]{1,0:T(8,128)(2,1)S(1)}, ...), condition=%wide.region_8.9_spmd.clone, body=%wide.region_4.8_spmd.clone.sunk | while | flops 268963936 | bytes 10520344 | solution.py:104
  32.0 6.4 %conditional.3 = (f32[1,224,2048]{2,1,0:T(8,128)S(1)}, f32[1,224]{1,0:T(1,128)S(1)}, bf16[32,2048]{1,0:T(8,128)(2,1)S(1)}) conditional(s32[]{:T(128)} %convert_element_type.47, (f32[1,224,2048]{2,1,0:T(8,128)S(1)}, f32[1,224]{1,0:T(1,128)S(1)}) %tuple.68, (pred[]{:T(512)}, f32[1,2048]{1,0:T(1,128)S(1)}, bf16[1,2048,2048]{2,1,0:T(8,128)(2,1)}, ...), branch_computations={%region_5.5_spmd, %region_6.7_spmd} | conditional | flops 268959840 | bytes 9987569 | solution.py:95
  42.9 6.5 %conditional.3 = (f32[1,224,2048]{2,1,0:T(8,128)S(1)}, f32[1,224]{1,0:T(1,128)S(1)}, bf16[32,2048]{1,0:T(8,128)(2,1)S(1)}) conditional(s32[]{:T(128)} %convert_element_type.47, (f32[1,224,2048]{2,1,0:T(8,128)S(1)}, f32[1,224]{1,0:T(1,128)S(1)}) %tuple.68, (pred[]{:T(512)}, f32[1,2048]{1,0:T(1,128)S(1)}, bf16[1,2048,2048]{2,1,0:T(8,128)(2,1)}, ...), branch_computations={%region_5.5_spmd, %region_6.7_spmd} | conditional | flops 268959840 | bytes 9987569 | solution.py:95
  56.2 6.5 %conditional.3 = (f32[1,224,2048]{2,1,0:T(8,128)S(1)}, f32[1,224]{1,0:T(1,128)S(1)}, bf16[32,2048]{1,0:T(8,128)(2,1)S(1)}) conditional(s32[]{:T(128)} %convert_element_type.47, (f32[1,224,2048]{2,1,0:T(8,128)S(1)}, f32[1,224]{1,0:T(1,128)S(1)}) %tuple.68, (pred[]{:T(512)}, f32[1,2048]{1,0:T(1,128)S(1)}, bf16[1,2048,2048]{2,1,0:T(8,128)(2,1)}, ...), branch_computations={%region_5.5_spmd, %region_6.7_spmd} | conditional | flops 268959840 | bytes 9987569 | solution.py:95
  67.2 6.5 %conditional.3 = (f32[1,224,2048]{2,1,0:T(8,128)S(1)}, f32[1,224]{1,0:T(1,128)S(1)}, bf16[32,2048]{1,0:T(8,128)(2,1)S(1)}) conditional(s32[]{:T(128)} %convert_element_type.47, (f32[1,224,2048]{2,1,0:T(8,128)S(1)}, f32[1,224]{1,0:T(1,128)S(1)}) %tuple.68, (pred[]{:T(512)}, f32[1,2048]{1,0:T(1,128)S(1)}, bf16[1,2048,2048]{2,1,0:T(8,128)(2,1)}, ...), branch_computations={%region_5.5_spmd, %region_6.7_spmd} | conditional | flops 268959840 | bytes 9987569 | solution.py:95
  80.6 6.4 %conditional.3 = (f32[1,224,2048]{2,1,0:T(8,128)S(1)}, f32[1,224]{1,0:T(1,128)S(1)}, bf16[32,2048]{1,0:T(8,128)(2,1)S(1)}) conditional(s32[]{:T(128)} %convert_element_type.47, (f32[1,224,2048]{2,1,0:T(8,128)S(1)}, f32[1,224]{1,0:T(1,128)S(1)}) %tuple.68, (pred[]{:T(512)}, f32[1,2048]{1,0:T(1,128)S(1)}, bf16[1,2048,2048]{2,1,0:T(8,128)(2,1)}, ...), branch_computations={%region_5.5_spmd, %region_6.7_spmd} | conditional | flops 268959840 | bytes 9987569 | solution.py:95
  94.1 6.5 %conditional.3 = (f32[1,224,2048]{2,1,0:T(8,128)S(1)}, f32[1,224]{1,0:T(1,128)S(1)}, bf16[32,2048]{1,0:T(8,128)(2,1)S(1)}) conditional(s32[]{:T(128)} %convert_element_type.47, (f32[1,224,2048]{2,1,0:T(8,128)S(1)}, f32[1,224]{1,0:T(1,128)S(1)}) %tuple.68, (pred[]{:T(512)}, f32[1,2048]{1,0:T(1,128)S(1)}, bf16[1,2048,2048]{2,1,0:T(8,128)(2,1)}, ...), branch_computations={%region_5.5_spmd, %region_6.7_spmd} | conditional | flops 268959840 | bytes 9987569 | solution.py:95
  107.5 6.5 %conditional.3 = (f32[1,224,2048]{2,1,0:T(8,128)S(1)}, f32[1,224]{1,0:T(1,128)S(1)}, bf16[32,2048]{1,0:T(8,128)(2,1)S(1)}) conditional(s32[]{:T(128)} %convert_element_type.47, (f32[1,224,2048]{2,1,0:T(8,128)S(1)}, f32[1,224]{1,0:T(1,128)S(1)}) %tuple.68, (pred[]{:T(512)}, f32[1,2048]{1,0:T(1,128)S(1)}, bf16[1,2048,2048]{2,1,0:T(8,128)(2,1)}, ...), branch_computations={%region_5.5_spmd, %region_6.7_spmd} | conditional | flops 268959840 | bytes 9987569 | solution.py:95
  121.1 11.7 %collective-permute-start = (bf16[32,2048]{1,0:T(8,128)(2,1)S(1)}, bf16[32,2048]{1,0:T(8,128)(2,1)S(1)}, u32[]{:S(2)}, u32[]{:S(2)}) collective-permute-start(bf16[32,2048]{1,0:T(8,128)(2,1)S(1)} %get-tuple-element.433), channel_id=1, source_target_pairs={{0,1},{1,2},{2,3},{3,4},{4,5},{5,6},{6,7},{7,8},{8,9},{9,10},{10,1... | collective-permute-start | bytes 393224 | tf_op jit(solution)/shard_map/while/body/eval_jaxpr/ppermute | solution.py:14
  141.5 11.8 %collective-permute-start = (bf16[32,2048]{1,0:T(8,128)(2,1)S(1)}, bf16[32,2048]{1,0:T(8,128)(2,1)S(1)}, u32[]{:S(2)}, u32[]{:S(2)}) collective-permute-start(bf16[32,2048]{1,0:T(8,128)(2,1)S(1)} %get-tuple-element.433), channel_id=1, source_target_pairs={{0,1},{1,2},{2,3},{3,4},{4,5},{5,6},{6,7},{7,8},{8,9},{9,10},{10,1... | collective-permute-start | bytes 393224 | tf_op jit(solution)/shard_map/while/body/eval_jaxpr/ppermute | solution.py:14
  162.0 7.3 %collective-permute-start = (bf16[32,2048]{1,0:T(8,128)(2,1)S(1)}, bf16[32,2048]{1,0:T(8,128)(2,1)S(1)}, u32[]{:S(2)}, u32[]{:S(2)}) collective-permute-start(bf16[32,2048]{1,0:T(8,128)(2,1)S(1)} %get-tuple-element.433), channel_id=1, source_target_pairs={{0,1},{1,2},{2,3},{3,4},{4,5},{5,6},{6,7},{7,8},{8,9},{9,10},{10,1... | collective-permute-start | bytes 393224 | tf_op jit(solution)/shard_map/while/body/eval_jaxpr/ppermute | solution.py:14
  170.9 6.2 %collective-permute-start = (bf16[32,2048]{1,0:T(8,128)(2,1)S(1)}, bf16[32,2048]{1,0:T(8,128)(2,1)S(1)}, u32[]{:S(2)}, u32[]{:S(2)}) collective-permute-start(bf16[32,2048]{1,0:T(8,128)(2,1)S(1)} %get-tuple-element.433), channel_id=1, source_target_pairs={{0,1},{1,2},{2,3},{3,4},{4,5},{5,6},{6,7},{7,8},{8,9},{9,10},{10,1... | collective-permute-start | bytes 393224 | tf_op jit(solution)/shard_map/while/body/eval_jaxpr/ppermute | solution.py:14
  178.8 12.7 %collective-permute-start = (bf16[32,2048]{1,0:T(8,128)(2,1)S(1)}, bf16[32,2048]{1,0:T(8,128)(2,1)S(1)}, u32[]{:S(2)}, u32[]{:S(2)}) collective-permute-start(bf16[32,2048]{1,0:T(8,128)(2,1)S(1)} %get-tuple-element.433), channel_id=1, source_target_pairs={{0,1},{1,2},{2,3},{3,4},{4,5},{5,6},{6,7},{7,8},{8,9},{9,10},{10,1... | collective-permute-start | bytes 393224 | tf_op jit(solution)/shard_map/while/body/eval_jaxpr/ppermute | solution.py:14
  193.2 6.2 %collective-permute-start = (bf16[32,2048]{1,0:T(8,128)(2,1)S(1)}, bf16[32,2048]{1,0:T(8,128)(2,1)S(1)}, u32[]{:S(2)}, u32[]{:S(2)}) collective-permute-start(bf16[32,2048]{1,0:T(8,128)(2,1)S(1)} %get-tuple-element.433), channel_id=1, source_target_pairs={{0,1},{1,2},{2,3},{3,4},{4,5},{5,6},{6,7},{7,8},{8,9},{9,10},{10,1... | collective-permute-start | bytes 393224 | tf_op jit(solution)/shard_map/while/body/eval_jaxpr/ppermute | solution.py:14
  216.9 6.7 %collective-permute-start = (bf16[32,2048]{1,0:T(8,128)(2,1)S(1)}, bf16[32,2048]{1,0:T(8,128)(2,1)S(1)}, u32[]{:S(2)}, u32[]{:S(2)}) collective-permute-start(bf16[32,2048]{1,0:T(8,128)(2,1)S(1)} %get-tuple-element.433), channel_id=1, source_target_pairs={{0,1},{1,2},{2,3},{3,4},{4,5},{5,6},{6,7},{7,8},{8,9},{9,10},{10,1... | collective-permute-start | bytes 393224 | tf_op jit(solution)/shard_map/while/body/eval_jaxpr/ppermute | solution.py:14
  225.2 6.2 %collective-permute-start = (bf16[32,2048]{1,0:T(8,128)(2,1)S(1)}, bf16[32,2048]{1,0:T(8,128)(2,1)S(1)}, u32[]{:S(2)}, u32[]{:S(2)}) collective-permute-start(bf16[32,2048]{1,0:T(8,128)(2,1)S(1)} %get-tuple-element.433), channel_id=1, source_target_pairs={{0,1},{1,2},{2,3},{3,4},{4,5},{5,6},{6,7},{7,8},{8,9},{9,10},{10,1... | collective-permute-start | bytes 393224 | tf_op jit(solution)/shard_map/while/body/eval_jaxpr/ppermute | solution.py:14
  233.2 6.2 %collective-permute-start = (bf16[32,2048]{1,0:T(8,128)(2,1)S(1)}, bf16[32,2048]{1,0:T(8,128)(2,1)S(1)}, u32[]{:S(2)}, u32[]{:S(2)}) collective-permute-start(bf16[32,2048]{1,0:T(8,128)(2,1)S(1)} %get-tuple-element.433), channel_id=1, source_target_pairs={{0,1},{1,2},{2,3},{3,4},{4,5},{5,6},{6,7},{7,8},{8,9},{9,10},{10,1... | collective-permute-start | bytes 393224 | tf_op jit(solution)/shard_map/while/body/eval_jaxpr/ppermute | solution.py:14
  249.0 7.6 %collective-permute-start = (bf16[32,2048]{1,0:T(8,128)(2,1)S(1)}, bf16[32,2048]{1,0:T(8,128)(2,1)S(1)}, u32[]{:S(2)}, u32[]{:S(2)}) collective-permute-start(bf16[32,2048]{1,0:T(8,128)(2,1)S(1)} %get-tuple-element.433), channel_id=1, source_target_pairs={{0,1},{1,2},{2,3},{3,4},{4,5},{5,6},{6,7},{7,8},{8,9},{9,10},{10,1... | collective-permute-start | bytes 393224 | tf_op jit(solution)/shard_map/while/body/eval_jaxpr/ppermute | solution.py:14
  257.6 76.6 %psum.7 = f32[224]{0:T(256)S(1)} all-reduce(f32[224]{0:T(256)S(1)} %bitcast.57), channel_id=1, replica_groups=mesh['groups'=2,'tm'=16] {'tm'}, use_global_device_ids=true, to_apply=%region_9.10 | all-reduce | flops 224 | bytes 1792 | tf_op jit(solution)/shard_map/psum | solution.py:106
  (140 shorter events, 147.1 us)
Async XLA Ops:
  0.6 4.2 %collective-permute-start.1 = (f32[64,2048]{1,0:T(8,128)}, f32[64,2048]{1,0:T(8,128)S(1)}, u32[]{:S(2)}, u32[]{:S(2)}) collective-permute-start(f32[64,2048]{1,0:T(8,128)} %bitcast.54), channel_id=1, source_target_pairs={{0,1},{1,2},{2,3},{3,4},{4,5},{5,6},{6,7},{7,8},{8,9},{9,10},{10,1... | collective-permute-start | bytes 1572872 | tf_op jit(solution)/shard_map/ppermute | solution.py:14
  38.5 3.7 %collective-permute-start = (bf16[32,2048]{1,0:T(8,128)(2,1)S(1)}, bf16[32,2048]{1,0:T(8,128)(2,1)S(1)}, u32[]{:S(2)}, u32[]{:S(2)}) collective-permute-start(bf16[32,2048]{1,0:T(8,128)(2,1)S(1)} %get-tuple-element.433), channel_id=1, source_target_pairs={{0,1},{1,2},{2,3},{3,4},{4,5},{5,6},{6,7},{7,8},{8,9},{9,10},{10,1... | collective-permute-start | bytes 393224 | tf_op jit(solution)/shard_map/while/body/eval_jaxpr/ppermute | solution.py:14
  49.4 6.1 %collective-permute-start = (bf16[32,2048]{1,0:T(8,128)(2,1)S(1)}, bf16[32,2048]{1,0:T(8,128)(2,1)S(1)}, u32[]{:S(2)}, u32[]{:S(2)}) collective-permute-start(bf16[32,2048]{1,0:T(8,128)(2,1)S(1)} %get-tuple-element.433), channel_id=1, source_target_pairs={{0,1},{1,2},{2,3},{3,4},{4,5},{5,6},{6,7},{7,8},{8,9},{9,10},{10,1... | collective-permute-start | bytes 393224 | tf_op jit(solution)/shard_map/while/body/eval_jaxpr/ppermute | solution.py:14
  62.7 3.9 %collective-permute-start = (bf16[32,2048]{1,0:T(8,128)(2,1)S(1)}, bf16[32,2048]{1,0:T(8,128)(2,1)S(1)}, u32[]{:S(2)}, u32[]{:S(2)}) collective-permute-start(bf16[32,2048]{1,0:T(8,128)(2,1)S(1)} %get-tuple-element.433), channel_id=1, source_target_pairs={{0,1},{1,2},{2,3},{3,4},{4,5},{5,6},{6,7},{7,8},{8,9},{9,10},{10,1... | collective-permute-start | bytes 393224 | tf_op jit(solution)/shard_map/while/body/eval_jaxpr/ppermute | solution.py:14
  73.8 6.2 %collective-permute-start = (bf16[32,2048]{1,0:T(8,128)(2,1)S(1)}, bf16[32,2048]{1,0:T(8,128)(2,1)S(1)}, u32[]{:S(2)}, u32[]{:S(2)}) collective-permute-start(bf16[32,2048]{1,0:T(8,128)(2,1)S(1)} %get-tuple-element.433), channel_id=1, source_target_pairs={{0,1},{1,2},{2,3},{3,4},{4,5},{5,6},{6,7},{7,8},{8,9},{9,10},{10,1... | collective-permute-start | bytes 393224 | tf_op jit(solution)/shard_map/while/body/eval_jaxpr/ppermute | solution.py:14
  87.1 6.4 %collective-permute-start = (bf16[32,2048]{1,0:T(8,128)(2,1)S(1)}, bf16[32,2048]{1,0:T(8,128)(2,1)S(1)}, u32[]{:S(2)}, u32[]{:S(2)}) collective-permute-start(bf16[32,2048]{1,0:T(8,128)(2,1)S(1)} %get-tuple-element.433), channel_id=1, source_target_pairs={{0,1},{1,2},{2,3},{3,4},{4,5},{5,6},{6,7},{7,8},{8,9},{9,10},{10,1... | collective-permute-start | bytes 393224 | tf_op jit(solution)/shard_map/while/body/eval_jaxpr/ppermute | solution.py:14
  100.6 6.2 %collective-permute-start = (bf16[32,2048]{1,0:T(8,128)(2,1)S(1)}, bf16[32,2048]{1,0:T(8,128)(2,1)S(1)}, u32[]{:S(2)}, u32[]{:S(2)}) collective-permute-start(bf16[32,2048]{1,0:T(8,128)(2,1)S(1)} %get-tuple-element.433), channel_id=1, source_target_pairs={{0,1},{1,2},{2,3},{3,4},{4,5},{5,6},{6,7},{7,8},{8,9},{9,10},{10,1... | collective-permute-start | bytes 393224 | tf_op jit(solution)/shard_map/while/body/eval_jaxpr/ppermute | solution.py:14
  114.0 6.4 %collective-permute-start = (bf16[32,2048]{1,0:T(8,128)(2,1)S(1)}, bf16[32,2048]{1,0:T(8,128)(2,1)S(1)}, u32[]{:S(2)}, u32[]{:S(2)}) collective-permute-start(bf16[32,2048]{1,0:T(8,128)(2,1)S(1)} %get-tuple-element.433), channel_id=1, source_target_pairs={{0,1},{1,2},{2,3},{3,4},{4,5},{5,6},{6,7},{7,8},{8,9},{9,10},{10,1... | collective-permute-start | bytes 393224 | tf_op jit(solution)/shard_map/while/body/eval_jaxpr/ppermute | solution.py:14
  121.1 12.7 %collective-permute-start = (bf16[32,2048]{1,0:T(8,128)(2,1)S(1)}, bf16[32,2048]{1,0:T(8,128)(2,1)S(1)}, u32[]{:S(2)}, u32[]{:S(2)}) collective-permute-start(bf16[32,2048]{1,0:T(8,128)(2,1)S(1)} %get-tuple-element.433), channel_id=1, source_target_pairs={{0,1},{1,2},{2,3},{3,4},{4,5},{5,6},{6,7},{7,8},{8,9},{9,10},{10,1... | collective-permute-start | bytes 393224 | tf_op jit(solution)/shard_map/while/body/eval_jaxpr/ppermute | solution.py:14
  134.5 6.3 %collective-permute-start = (bf16[32,2048]{1,0:T(8,128)(2,1)S(1)}, bf16[32,2048]{1,0:T(8,128)(2,1)S(1)}, u32[]{:S(2)}, u32[]{:S(2)}) collective-permute-start(bf16[32,2048]{1,0:T(8,128)(2,1)S(1)} %get-tuple-element.433), channel_id=1, source_target_pairs={{0,1},{1,2},{2,3},{3,4},{4,5},{5,6},{6,7},{7,8},{8,9},{9,10},{10,1... | collective-permute-start | bytes 393224 | tf_op jit(solution)/shard_map/while/body/eval_jaxpr/ppermute | solution.py:14
  141.5 12.8 %collective-permute-start = (bf16[32,2048]{1,0:T(8,128)(2,1)S(1)}, bf16[32,2048]{1,0:T(8,128)(2,1)S(1)}, u32[]{:S(2)}, u32[]{:S(2)}) collective-permute-start(bf16[32,2048]{1,0:T(8,128)(2,1)S(1)} %get-tuple-element.433), channel_id=1, source_target_pairs={{0,1},{1,2},{2,3},{3,4},{4,5},{5,6},{6,7},{7,8},{8,9},{9,10},{10,1... | collective-permute-start | bytes 393224 | tf_op jit(solution)/shard_map/while/body/eval_jaxpr/ppermute | solution.py:14
  155.0 6.3 %collective-permute-start = (bf16[32,2048]{1,0:T(8,128)(2,1)S(1)}, bf16[32,2048]{1,0:T(8,128)(2,1)S(1)}, u32[]{:S(2)}, u32[]{:S(2)}) collective-permute-start(bf16[32,2048]{1,0:T(8,128)(2,1)S(1)} %get-tuple-element.433), channel_id=1, source_target_pairs={{0,1},{1,2},{2,3},{3,4},{4,5},{5,6},{6,7},{7,8},{8,9},{9,10},{10,1... | collective-permute-start | bytes 393224 | tf_op jit(solution)/shard_map/while/body/eval_jaxpr/ppermute | solution.py:14
  162.0 8.2 %collective-permute-start = (bf16[32,2048]{1,0:T(8,128)(2,1)S(1)}, bf16[32,2048]{1,0:T(8,128)(2,1)S(1)}, u32[]{:S(2)}, u32[]{:S(2)}) collective-permute-start(bf16[32,2048]{1,0:T(8,128)(2,1)S(1)} %get-tuple-element.433), channel_id=1, source_target_pairs={{0,1},{1,2},{2,3},{3,4},{4,5},{5,6},{6,7},{7,8},{8,9},{9,10},{10,1... | collective-permute-start | bytes 393224 | tf_op jit(solution)/shard_map/while/body/eval_jaxpr/ppermute | solution.py:14
  170.9 7.2 %collective-permute-start = (bf16[32,2048]{1,0:T(8,128)(2,1)S(1)}, bf16[32,2048]{1,0:T(8,128)(2,1)S(1)}, u32[]{:S(2)}, u32[]{:S(2)}) collective-permute-start(bf16[32,2048]{1,0:T(8,128)(2,1)S(1)} %get-tuple-element.433), channel_id=1, source_target_pairs={{0,1},{1,2},{2,3},{3,4},{4,5},{5,6},{6,7},{7,8},{8,9},{9,10},{10,1... | collective-permute-start | bytes 393224 | tf_op jit(solution)/shard_map/while/body/eval_jaxpr/ppermute | solution.py:14
  178.8 13.7 %collective-permute-start = (bf16[32,2048]{1,0:T(8,128)(2,1)S(1)}, bf16[32,2048]{1,0:T(8,128)(2,1)S(1)}, u32[]{:S(2)}, u32[]{:S(2)}) collective-permute-start(bf16[32,2048]{1,0:T(8,128)(2,1)S(1)} %get-tuple-element.433), channel_id=1, source_target_pairs={{0,1},{1,2},{2,3},{3,4},{4,5},{5,6},{6,7},{7,8},{8,9},{9,10},{10,1... | collective-permute-start | bytes 393224 | tf_op jit(solution)/shard_map/while/body/eval_jaxpr/ppermute | solution.py:14
  193.2 7.2 %collective-permute-start = (bf16[32,2048]{1,0:T(8,128)(2,1)S(1)}, bf16[32,2048]{1,0:T(8,128)(2,1)S(1)}, u32[]{:S(2)}, u32[]{:S(2)}) collective-permute-start(bf16[32,2048]{1,0:T(8,128)(2,1)S(1)} %get-tuple-element.433), channel_id=1, source_target_pairs={{0,1},{1,2},{2,3},{3,4},{4,5},{5,6},{6,7},{7,8},{8,9},{9,10},{10,1... | collective-permute-start | bytes 393224 | tf_op jit(solution)/shard_map/while/body/eval_jaxpr/ppermute | solution.py:14
  201.1 7.2 %collective-permute-start = (bf16[32,2048]{1,0:T(8,128)(2,1)S(1)}, bf16[32,2048]{1,0:T(8,128)(2,1)S(1)}, u32[]{:S(2)}, u32[]{:S(2)}) collective-permute-start(bf16[32,2048]{1,0:T(8,128)(2,1)S(1)} %get-tuple-element.433), channel_id=1, source_target_pairs={{0,1},{1,2},{2,3},{3,4},{4,5},{5,6},{6,7},{7,8},{8,9},{9,10},{10,1... | collective-permute-start | bytes 393224 | tf_op jit(solution)/shard_map/while/body/eval_jaxpr/ppermute | solution.py:14
  209.0 7.2 %collective-permute-start = (bf16[32,2048]{1,0:T(8,128)(2,1)S(1)}, bf16[32,2048]{1,0:T(8,128)(2,1)S(1)}, u32[]{:S(2)}, u32[]{:S(2)}) collective-permute-start(bf16[32,2048]{1,0:T(8,128)(2,1)S(1)} %get-tuple-element.433), channel_id=1, source_target_pairs={{0,1},{1,2},{2,3},{3,4},{4,5},{5,6},{6,7},{7,8},{8,9},{9,10},{10,1... | collective-permute-start | bytes 393224 | tf_op jit(solution)/shard_map/while/body/eval_jaxpr/ppermute | solution.py:14
  216.9 7.6 %collective-permute-start = (bf16[32,2048]{1,0:T(8,128)(2,1)S(1)}, bf16[32,2048]{1,0:T(8,128)(2,1)S(1)}, u32[]{:S(2)}, u32[]{:S(2)}) collective-permute-start(bf16[32,2048]{1,0:T(8,128)(2,1)S(1)} %get-tuple-element.433), channel_id=1, source_target_pairs={{0,1},{1,2},{2,3},{3,4},{4,5},{5,6},{6,7},{7,8},{8,9},{9,10},{10,1... | collective-permute-start | bytes 393224 | tf_op jit(solution)/shard_map/while/body/eval_jaxpr/ppermute | solution.py:14
  225.2 7.2 %collective-permute-start = (bf16[32,2048]{1,0:T(8,128)(2,1)S(1)}, bf16[32,2048]{1,0:T(8,128)(2,1)S(1)}, u32[]{:S(2)}, u32[]{:S(2)}) collective-permute-start(bf16[32,2048]{1,0:T(8,128)(2,1)S(1)} %get-tuple-element.433), channel_id=1, source_target_pairs={{0,1},{1,2},{2,3},{3,4},{4,5},{5,6},{6,7},{7,8},{8,9},{9,10},{10,1... | collective-permute-start | bytes 393224 | tf_op jit(solution)/shard_map/while/body/eval_jaxpr/ppermute | solution.py:14
  233.2 7.2 %collective-permute-start = (bf16[32,2048]{1,0:T(8,128)(2,1)S(1)}, bf16[32,2048]{1,0:T(8,128)(2,1)S(1)}, u32[]{:S(2)}, u32[]{:S(2)}) collective-permute-start(bf16[32,2048]{1,0:T(8,128)(2,1)S(1)} %get-tuple-element.433), channel_id=1, source_target_pairs={{0,1},{1,2},{2,3},{3,4},{4,5},{5,6},{6,7},{7,8},{8,9},{9,10},{10,1... | collective-permute-start | bytes 393224 | tf_op jit(solution)/shard_map/while/body/eval_jaxpr/ppermute | solution.py:14
  241.1 7.2 %collective-permute-start = (bf16[32,2048]{1,0:T(8,128)(2,1)S(1)}, bf16[32,2048]{1,0:T(8,128)(2,1)S(1)}, u32[]{:S(2)}, u32[]{:S(2)}) collective-permute-start(bf16[32,2048]{1,0:T(8,128)(2,1)S(1)} %get-tuple-element.433), channel_id=1, source_target_pairs={{0,1},{1,2},{2,3},{3,4},{4,5},{5,6},{6,7},{7,8},{8,9},{9,10},{10,1... | collective-permute-start | bytes 393224 | tf_op jit(solution)/shard_map/while/body/eval_jaxpr/ppermute | solution.py:14
  249.0 8.6 %collective-permute-start = (bf16[32,2048]{1,0:T(8,128)(2,1)S(1)}, bf16[32,2048]{1,0:T(8,128)(2,1)S(1)}, u32[]{:S(2)}, u32[]{:S(2)}) collective-permute-start(bf16[32,2048]{1,0:T(8,128)(2,1)S(1)} %get-tuple-element.433), channel_id=1, source_target_pairs={{0,1},{1,2},{2,3},{3,4},{4,5},{5,6},{6,7},{7,8},{8,9},{9,10},{10,1... | collective-permute-start | bytes 393224 | tf_op jit(solution)/shard_map/while/body/eval_jaxpr/ppermute | solution.py:14
  257.5 77.2 %copy-start = (f32[1,224,2048]{2,1,0:T(8,128)}, f32[1,224,2048]{2,1,0:T(8,128)S(1)}, u32[]{:S(2)}) copy-start(f32[1,224,2048]{2,1,0:T(8,128)S(1)} %get-tuple-element.273) | copy-start | bytes 5505028
where the time goes:
time: 336 us; the launch traced here: 335 us
  starting transfers between devices  146 us (43%)
  blocking collectives  76.6 us (23%)
  matrix products  61.3 us (18%)
  other arithmetic  24.4 us (7%)
  waiting for transfers between devices  21.1 us (6%)
    ppermute x23, starting transfers between devices, shifted(): lax.ppermute(value, axis, [(source, source + steps) for source in range(i...  146 us
    psum x1, blocking collectives, per_device(): log_scale = lax.psum(local_log, 'tm') / (tm_count * local_slices - 1)  76.6 us
    dot_general x7, matrix products, push_forward(): jnp.dot(weighted, kernel, preferred_element_type=jnp.float32)  35.2 us
    dot_general x4, matrix products, one_block(): lax.dot_general(segment, target, (((0,), (0,)), ((), ())), precision=lax....  26.1 us
    ppermute x23, waiting for transfers between devices, shifted(): lax.ppermute(value, axis, [(source, source + steps) for source in range(i...  21.1 us
    convert_element_type x22, other arithmetic, per_device(): (jnp.arange(point_count, dtype=jnp.int32)[None, :] < supports[:, None]).a...  14.4 us
    convert_element_type x7, other arithmetic, section(): outgoing = (message * block_pot[local_slices - 1]).astype(jnp.bfloat16)  7.46 us
  transfers between devices with their start and end apart: 23, of which 22 were waited for; matrix products, arithmetic and copies ran while one was open for 0% of the time, Pallas kernels for 0%

commit v1 on v0

--- a/solution.py
+++ b/solution.py
@@ -6,6 +6,11 @@
 MICRO = 32
 A_DECAY = 0.8
 EPS_SCALE = 0.05
+
+
+def use_points(arr_in):
+    mixed_arr = lax.all_gather(arr_in, "tm").sum(axis=0)
+    return mixed_arr
 
 
 def shifted(value, axis, steps):
@@ -103,7 +108,7 @@
     )
     unused, messages, log_parts = lax.fori_loop(0, phase_count, advance, initial)
     local_log = jnp.sum(log_parts, axis=0)
-    log_scale = lax.psum(local_log, "tm") / (tm_count * local_slices - 1)
+    log_scale = use_points(local_log) / (tm_count * local_slices - 1)
     return (messages, log_scale)
 
 

time: 336 us -> 324 us (0.964)
  blocking collectives: 76.6 us -> 64.3 us
    psum x1 -> x0, blocking collectives: 76.6 us -> none  [per_device(): log_scale = lax.psum(local_log, 'tm') / (tm_count * local_slices - 1)]
    all_gather x0 -> x1, blocking collectives: none -> 64.3 us  [use_points(): mixed_arr = lax.all_gather(arr_in, 'tm').sum(axis=0)]
where the time goes in v1:
time: 324 us; the launch traced here: 322 us
  starting transfers between devices  146 us (45%)
  blocking collectives  64.3 us (20%)
  matrix products  61.3 us (19%)
  other arithmetic  24.5 us (8%)
  waiting for transfers between devices  21.1 us (7%)
    ppermute x23, starting transfers between devices, shifted(): lax.ppermute(value, axis, [(source, source + steps) for source in range(i...  146 us
    all_gather x1, blocking collectives, use_points(): mixed_arr = lax.all_gather(arr_in, 'tm').sum(axis=0)  64.3 us
    dot_general x7, matrix products, push_forward(): jnp.dot(weighted, kernel, preferred_element_type=jnp.float32)  35.2 us
    dot_general x4, matrix products, one_block(): lax.dot_general(segment, target, (((0,), (0,)), ((), ())), precision=lax....  26.1 us
    ppermute x23, waiting for transfers between devices, shifted(): lax.ppermute(value, axis, [(source, source + steps) for source in range(i...  21.1 us
    convert_element_type x22, other arithmetic, per_device(): (jnp.arange(point_count, dtype=jnp.int32)[None, :] < supports[:, None]).a...  14.4 us
    convert_element_type x7, other arithmetic, section(): outgoing = (message * block_pot[local_slices - 1]).astype(jnp.bfloat16)  7.46 us
  transfers between devices with their start and end apart: 23, of which 22 were waited for; matrix products, arithmetic and copies ran while one was open for 0% of the time, Pallas kernels for 0%

profile of v1, /device:TPU:0, one launch (start us, length us, event | category | flops | bytes accessed | tf_op | source)
XLA Modules:
  0.0 322.5 jit_solution(1200826836535629276)
XLA Ops:
  4.9 26.2 %while.35 = (s32[]{:T(128)}, bf16[4,512,2048]{2,1,0:T(8,128)(2,1)}, f32[2048]{0:T(1024)S(1)}, f32[4,64,512]{2,1,0:T(8,128)S(1)}, f32[64,2048]{1,0:T(8,128)}, /*index=5*/s32[]{:T(128)}) while((s32[]{:T(128)}, bf16[4,512,2048]{2,1,0:T(8,128)(2,1)}, f32[2048]{0:T(1024)S(1)}, f32[4,64,512]{2,1,0:T(8,128)S(1)}, f32[64,2048]{1,0:T(8,128)}, ...), condition=%wide.region_3.0_spmd, body=%wide.region_1.3_spmd.sunk | while | flops 810614784 | bytes 2901065 | solution.py:45
  4.9 6.5 %fusion.26 = bf16[4,512,2048]{2,1,0:T(8,128)(2,1)} fusion(bf16[4,512,2048]{2,1,0:T(8,128)(2,1)} %get-tuple-element.449, s32[]{:T(128)} %get-tuple-element.448, f32[64,2048]{1,0:T(8,128)} %get-tuple-element.458, f32[512]{0:T(512)S(1)} %broadcast_multiply_fusion.3, f32[2048]{0:T(1024)S(1)} %get-tuple-element.456, f32[4,64,512]{2,1,0:T(8,128)S(1)} %get-tuple-element.457), kind=kOutput, calls=%fused_computation.3.clone.1 | convolution fusion | flops 810549248 | bytes 2763776 | tf_op jit(solution)/shard_map/while/body/eval_jaxpr/while/body/eval_jaxpr/dot_general | solution.py:32
  11.5 6.5 %fusion.26 = bf16[4,512,2048]{2,1,0:T(8,128)(2,1)} fusion(bf16[4,512,2048]{2,1,0:T(8,128)(2,1)} %get-tuple-element.449, s32[]{:T(128)} %get-tuple-element.448, f32[64,2048]{1,0:T(8,128)} %get-tuple-element.458, f32[512]{0:T(512)S(1)} %broadcast_multiply_fusion.3, f32[2048]{0:T(1024)S(1)} %get-tuple-element.456, f32[4,64,512]{2,1,0:T(8,128)S(1)} %get-tuple-element.457), kind=kOutput, calls=%fused_computation.3.clone.1 | convolution fusion | flops 810549248 | bytes 2763776 | tf_op jit(solution)/shard_map/while/body/eval_jaxpr/while/body/eval_jaxpr/dot_general | solution.py:32
  18.1 6.5 %fusion.26 = bf16[4,512,2048]{2,1,0:T(8,128)(2,1)} fusion(bf16[4,512,2048]{2,1,0:T(8,128)(2,1)} %get-tuple-element.449, s32[]{:T(128)} %get-tuple-element.448, f32[64,2048]{1,0:T(8,128)} %get-tuple-element.458, f32[512]{0:T(512)S(1)} %broadcast_multiply_fusion.3, f32[2048]{0:T(1024)S(1)} %get-tuple-element.456, f32[4,64,512]{2,1,0:T(8,128)S(1)} %get-tuple-element.457), kind=kOutput, calls=%fused_computation.3.clone.1 | convolution fusion | flops 810549248 | bytes 2763776 | tf_op jit(solution)/shard_map/while/body/eval_jaxpr/while/body/eval_jaxpr/dot_general | solution.py:32
  24.6 6.5 %fusion.26 = bf16[4,512,2048]{2,1,0:T(8,128)(2,1)} fusion(bf16[4,512,2048]{2,1,0:T(8,128)(2,1)} %get-tuple-element.449, s32[]{:T(128)} %get-tuple-element.448, f32[64,2048]{1,0:T(8,128)} %get-tuple-element.458, f32[512]{0:T(512)S(1)} %broadcast_multiply_fusion.3, f32[2048]{0:T(1024)S(1)} %get-tuple-element.456, f32[4,64,512]{2,1,0:T(8,128)S(1)} %get-tuple-element.457), kind=kOutput, calls=%fused_computation.3.clone.1 | convolution fusion | flops 810549248 | bytes 2763776 | tf_op jit(solution)/shard_map/while/body/eval_jaxpr/while/body/eval_jaxpr/dot_general | solution.py:32
  31.4 226.2 %while.36 = (s32[]{:T(128)}, bf16[32,2048]{1,0:T(8,128)(2,1)S(1)}, f32[1,224,2048]{2,1,0:T(8,128)S(1)}, f32[1,224]{1,0:T(1,128)S(1)}, s32[]{:T(128)}, /*index=5*...) while((s32[]{:T(128)}, bf16[32,2048]{1,0:T(8,128)(2,1)S(1)}, ...), condition=%wide.region_8.9_spmd.clone, body=%wide.region_4.8_spmd.clone.sunk | while | flops 268963936 | bytes 10520344 | solution.py:109
  32.0 6.4 %conditional.3 = (f32[1,224,2048]{2,1,0:T(8,128)S(1)}, f32[1,224]{1,0:T(1,128)S(1)}, bf16[32,2048]{1,0:T(8,128)(2,1)S(1)}) conditional(s32[]{:T(128)} %convert_element_type.47, (f32[1,224,2048]{2,1,0:T(8,128)S(1)}, f32[1,224]{1,0:T(1,128)S(1)}) %tuple.68, (pred[]{:T(512)}, f32[1,2048]{1,0:T(1,128)S(1)}, bf16[1,2048,2048]{2,1,0:T(8,128)(2,1)}, ...), branch_computations={%region_5.5_spmd, %region_6.7_spmd} | conditional | flops 268959840 | bytes 9987569 | solution.py:100
  42.9 6.5 %conditional.3 = (f32[1,224,2048]{2,1,0:T(8,128)S(1)}, f32[1,224]{1,0:T(1,128)S(1)}, bf16[32,2048]{1,0:T(8,128)(2,1)S(1)}) conditional(s32[]{:T(128)} %convert_element_type.47, (f32[1,224,2048]{2,1,0:T(8,128)S(1)}, f32[1,224]{1,0:T(1,128)S(1)}) %tuple.68, (pred[]{:T(512)}, f32[1,2048]{1,0:T(1,128)S(1)}, bf16[1,2048,2048]{2,1,0:T(8,128)(2,1)}, ...), branch_computations={%region_5.5_spmd, %region_6.7_spmd} | conditional | flops 268959840 | bytes 9987569 | solution.py:100
  56.2 6.5 %conditional.3 = (f32[1,224,2048]{2,1,0:T(8,128)S(1)}, f32[1,224]{1,0:T(1,128)S(1)}, bf16[32,2048]{1,0:T(8,128)(2,1)S(1)}) conditional(s32[]{:T(128)} %convert_element_type.47, (f32[1,224,2048]{2,1,0:T(8,128)S(1)}, f32[1,224]{1,0:T(1,128)S(1)}) %tuple.68, (pred[]{:T(512)}, f32[1,2048]{1,0:T(1,128)S(1)}, bf16[1,2048,2048]{2,1,0:T(8,128)(2,1)}, ...), branch_computations={%region_5.5_spmd, %region_6.7_spmd} | conditional | flops 268959840 | bytes 9987569 | solution.py:100
  67.2 6.5 %conditional.3 = (f32[1,224,2048]{2,1,0:T(8,128)S(1)}, f32[1,224]{1,0:T(1,128)S(1)}, bf16[32,2048]{1,0:T(8,128)(2,1)S(1)}) conditional(s32[]{:T(128)} %convert_element_type.47, (f32[1,224,2048]{2,1,0:T(8,128)S(1)}, f32[1,224]{1,0:T(1,128)S(1)}) %tuple.68, (pred[]{:T(512)}, f32[1,2048]{1,0:T(1,128)S(1)}, bf16[1,2048,2048]{2,1,0:T(8,128)(2,1)}, ...), branch_computations={%region_5.5_spmd, %region_6.7_spmd} | conditional | flops 268959840 | bytes 9987569 | solution.py:100
  80.6 6.4 %conditional.3 = (f32[1,224,2048]{2,1,0:T(8,128)S(1)}, f32[1,224]{1,0:T(1,128)S(1)}, bf16[32,2048]{1,0:T(8,128)(2,1)S(1)}) conditional(s32[]{:T(128)} %convert_element_type.47, (f32[1,224,2048]{2,1,0:T(8,128)S(1)}, f32[1,224]{1,0:T(1,128)S(1)}) %tuple.68, (pred[]{:T(512)}, f32[1,2048]{1,0:T(1,128)S(1)}, bf16[1,2048,2048]{2,1,0:T(8,128)(2,1)}, ...), branch_computations={%region_5.5_spmd, %region_6.7_spmd} | conditional | flops 268959840 | bytes 9987569 | solution.py:100
  94.1 6.5 %conditional.3 = (f32[1,224,2048]{2,1,0:T(8,128)S(1)}, f32[1,224]{1,0:T(1,128)S(1)}, bf16[32,2048]{1,0:T(8,128)(2,1)S(1)}) conditional(s32[]{:T(128)} %convert_element_type.47, (f32[1,224,2048]{2,1,0:T(8,128)S(1)}, f32[1,224]{1,0:T(1,128)S(1)}) %tuple.68, (pred[]{:T(512)}, f32[1,2048]{1,0:T(1,128)S(1)}, bf16[1,2048,2048]{2,1,0:T(8,128)(2,1)}, ...), branch_computations={%region_5.5_spmd, %region_6.7_spmd} | conditional | flops 268959840 | bytes 9987569 | solution.py:100
  107.5 6.5 %conditional.3 = (f32[1,224,2048]{2,1,0:T(8,128)S(1)}, f32[1,224]{1,0:T(1,128)S(1)}, bf16[32,2048]{1,0:T(8,128)(2,1)S(1)}) conditional(s32[]{:T(128)} %convert_element_type.47, (f32[1,224,2048]{2,1,0:T(8,128)S(1)}, f32[1,224]{1,0:T(1,128)S(1)}) %tuple.68, (pred[]{:T(512)}, f32[1,2048]{1,0:T(1,128)S(1)}, bf16[1,2048,2048]{2,1,0:T(8,128)(2,1)}, ...), branch_computations={%region_5.5_spmd, %region_6.7_spmd} | conditional | flops 268959840 | bytes 9987569 | solution.py:100
  121.1 11.7 %collective-permute-start = (bf16[32,2048]{1,0:T(8,128)(2,1)S(1)}, bf16[32,2048]{1,0:T(8,128)(2,1)S(1)}, u32[]{:S(2)}, u32[]{:S(2)}) collective-permute-start(bf16[32,2048]{1,0:T(8,128)(2,1)S(1)} %get-tuple-element.433), channel_id=1, source_target_pairs={{0,1},{1,2},{2,3},{3,4},{4,5},{5,6},{6,7},{7,8},{8,9},{9,10},{10,1... | collective-permute-start | bytes 393224 | tf_op jit(solution)/shard_map/while/body/eval_jaxpr/ppermute | solution.py:19
  141.5 11.8 %collective-permute-start = (bf16[32,2048]{1,0:T(8,128)(2,1)S(1)}, bf16[32,2048]{1,0:T(8,128)(2,1)S(1)}, u32[]{:S(2)}, u32[]{:S(2)}) collective-permute-start(bf16[32,2048]{1,0:T(8,128)(2,1)S(1)} %get-tuple-element.433), channel_id=1, source_target_pairs={{0,1},{1,2},{2,3},{3,4},{4,5},{5,6},{6,7},{7,8},{8,9},{9,10},{10,1... | collective-permute-start | bytes 393224 | tf_op jit(solution)/shard_map/while/body/eval_jaxpr/ppermute | solution.py:19
  162.0 7.3 %collective-permute-start = (bf16[32,2048]{1,0:T(8,128)(2,1)S(1)}, bf16[32,2048]{1,0:T(8,128)(2,1)S(1)}, u32[]{:S(2)}, u32[]{:S(2)}) collective-permute-start(bf16[32,2048]{1,0:T(8,128)(2,1)S(1)} %get-tuple-element.433), channel_id=1, source_target_pairs={{0,1},{1,2},{2,3},{3,4},{4,5},{5,6},{6,7},{7,8},{8,9},{9,10},{10,1... | collective-permute-start | bytes 393224 | tf_op jit(solution)/shard_map/while/body/eval_jaxpr/ppermute | solution.py:19
  170.9 6.2 %collective-permute-start = (bf16[32,2048]{1,0:T(8,128)(2,1)S(1)}, bf16[32,2048]{1,0:T(8,128)(2,1)S(1)}, u32[]{:S(2)}, u32[]{:S(2)}) collective-permute-start(bf16[32,2048]{1,0:T(8,128)(2,1)S(1)} %get-tuple-element.433), channel_id=1, source_target_pairs={{0,1},{1,2},{2,3},{3,4},{4,5},{5,6},{6,7},{7,8},{8,9},{9,10},{10,1... | collective-permute-start | bytes 393224 | tf_op jit(solution)/shard_map/while/body/eval_jaxpr/ppermute | solution.py:19
  178.8 12.7 %collective-permute-start = (bf16[32,2048]{1,0:T(8,128)(2,1)S(1)}, bf16[32,2048]{1,0:T(8,128)(2,1)S(1)}, u32[]{:S(2)}, u32[]{:S(2)}) collective-permute-start(bf16[32,2048]{1,0:T(8,128)(2,1)S(1)} %get-tuple-element.433), channel_id=1, source_target_pairs={{0,1},{1,2},{2,3},{3,4},{4,5},{5,6},{6,7},{7,8},{8,9},{9,10},{10,1... | collective-permute-start | bytes 393224 | tf_op jit(solution)/shard_map/while/body/eval_jaxpr/ppermute | solution.py:19
  193.2 6.2 %collective-permute-start = (bf16[32,2048]{1,0:T(8,128)(2,1)S(1)}, bf16[32,2048]{1,0:T(8,128)(2,1)S(1)}, u32[]{:S(2)}, u32[]{:S(2)}) collective-permute-start(bf16[32,2048]{1,0:T(8,128)(2,1)S(1)} %get-tuple-element.433), channel_id=1, source_target_pairs={{0,1},{1,2},{2,3},{3,4},{4,5},{5,6},{6,7},{7,8},{8,9},{9,10},{10,1... | collective-permute-start | bytes 393224 | tf_op jit(solution)/shard_map/while/body/eval_jaxpr/ppermute | solution.py:19
  216.9 6.7 %collective-permute-start = (bf16[32,2048]{1,0:T(8,128)(2,1)S(1)}, bf16[32,2048]{1,0:T(8,128)(2,1)S(1)}, u32[]{:S(2)}, u32[]{:S(2)}) collective-permute-start(bf16[32,2048]{1,0:T(8,128)(2,1)S(1)} %get-tuple-element.433), channel_id=1, source_target_pairs={{0,1},{1,2},{2,3},{3,4},{4,5},{5,6},{6,7},{7,8},{8,9},{9,10},{10,1... | collective-permute-start | bytes 393224 | tf_op jit(solution)/shard_map/while/body/eval_jaxpr/ppermute | solution.py:19
  225.2 6.2 %collective-permute-start = (bf16[32,2048]{1,0:T(8,128)(2,1)S(1)}, bf16[32,2048]{1,0:T(8,128)(2,1)S(1)}, u32[]{:S(2)}, u32[]{:S(2)}) collective-permute-start(bf16[32,2048]{1,0:T(8,128)(2,1)S(1)} %get-tuple-element.433), channel_id=1, source_target_pairs={{0,1},{1,2},{2,3},{3,4},{4,5},{5,6},{6,7},{7,8},{8,9},{9,10},{10,1... | collective-permute-start | bytes 393224 | tf_op jit(solution)/shard_map/while/body/eval_jaxpr/ppermute | solution.py:19
  233.2 6.2 %collective-permute-start = (bf16[32,2048]{1,0:T(8,128)(2,1)S(1)}, bf16[32,2048]{1,0:T(8,128)(2,1)S(1)}, u32[]{:S(2)}, u32[]{:S(2)}) collective-permute-start(bf16[32,2048]{1,0:T(8,128)(2,1)S(1)} %get-tuple-element.433), channel_id=1, source_target_pairs={{0,1},{1,2},{2,3},{3,4},{4,5},{5,6},{6,7},{7,8},{8,9},{9,10},{10,1... | collective-permute-start | bytes 393224 | tf_op jit(solution)/shard_map/while/body/eval_jaxpr/ppermute | solution.py:19
  249.0 7.6 %collective-permute-start = (bf16[32,2048]{1,0:T(8,128)(2,1)S(1)}, bf16[32,2048]{1,0:T(8,128)(2,1)S(1)}, u32[]{:S(2)}, u32[]{:S(2)}) collective-permute-start(bf16[32,2048]{1,0:T(8,128)(2,1)S(1)} %get-tuple-element.433), channel_id=1, source_target_pairs={{0,1},{1,2},{2,3},{3,4},{4,5},{5,6},{6,7},{7,8},{8,9},{9,10},{10,1... | collective-permute-start | bytes 393224 | tf_op jit(solution)/shard_map/while/body/eval_jaxpr/ppermute | solution.py:19
  257.6 64.3 %all-gather = f32[16,1,224]{2,1,0:T(1,128)S(1)} all-gather(f32[1,1,224]{2,1,0:T(1,128)S(1)} %bitcast.57), channel_id=1, replica_groups=mesh['groups'=2,'tm'=16] {'tm'}, dimensions={0}, use_global_device_ids=true | all-gather | bytes 15232 | tf_op jit(solution)/shard_map/all_gather | solution.py:12
  (141 shorter events, 147.1 us)
Async XLA Ops:
  0.6 4.2 %collective-permute-start.1 = (f32[64,2048]{1,0:T(8,128)}, f32[64,2048]{1,0:T(8,128)S(1)}, u32[]{:S(2)}, u32[]{:S(2)}) collective-permute-start(f32[64,2048]{1,0:T(8,128)} %bitcast.54), channel_id=1, source_target_pairs={{0,1},{1,2},{2,3},{3,4},{4,5},{5,6},{6,7},{7,8},{8,9},{9,10},{10,1... | collective-permute-start | bytes 1572872 | tf_op jit(solution)/shard_map/ppermute | solution.py:19
  38.5 3.7 %collective-permute-start = (bf16[32,2048]{1,0:T(8,128)(2,1)S(1)}, bf16[32,2048]{1,0:T(8,128)(2,1)S(1)}, u32[]{:S(2)}, u32[]{:S(2)}) collective-permute-start(bf16[32,2048]{1,0:T(8,128)(2,1)S(1)} %get-tuple-element.433), channel_id=1, source_target_pairs={{0,1},{1,2},{2,3},{3,4},{4,5},{5,6},{6,7},{7,8},{8,9},{9,10},{10,1... | collective-permute-start | bytes 393224 | tf_op jit(solution)/shard_map/while/body/eval_jaxpr/ppermute | solution.py:19
  49.4 6.1 %collective-permute-start = (bf16[32,2048]{1,0:T(8,128)(2,1)S(1)}, bf16[32,2048]{1,0:T(8,128)(2,1)S(1)}, u32[]{:S(2)}, u32[]{:S(2)}) collective-permute-start(bf16[32,2048]{1,0:T(8,128)(2,1)S(1)} %get-tuple-element.433), channel_id=1, source_target_pairs={{0,1},{1,2},{2,3},{3,4},{4,5},{5,6},{6,7},{7,8},{8,9},{9,10},{10,1... | collective-permute-start | bytes 393224 | tf_op jit(solution)/shard_map/while/body/eval_jaxpr/ppermute | solution.py:19
  62.7 3.9 %collective-permute-start = (bf16[32,2048]{1,0:T(8,128)(2,1)S(1)}, bf16[32,2048]{1,0:T(8,128)(2,1)S(1)}, u32[]{:S(2)}, u32[]{:S(2)}) collective-permute-start(bf16[32,2048]{1,0:T(8,128)(2,1)S(1)} %get-tuple-element.433), channel_id=1, source_target_pairs={{0,1},{1,2},{2,3},{3,4},{4,5},{5,6},{6,7},{7,8},{8,9},{9,10},{10,1... | collective-permute-start | bytes 393224 | tf_op jit(solution)/shard_map/while/body/eval_jaxpr/ppermute | solution.py:19
  73.8 6.2 %collective-permute-start = (bf16[32,2048]{1,0:T(8,128)(2,1)S(1)}, bf16[32,2048]{1,0:T(8,128)(2,1)S(1)}, u32[]{:S(2)}, u32[]{:S(2)}) collective-permute-start(bf16[32,2048]{1,0:T(8,128)(2,1)S(1)} %get-tuple-element.433), channel_id=1, source_target_pairs={{0,1},{1,2},{2,3},{3,4},{4,5},{5,6},{6,7},{7,8},{8,9},{9,10},{10,1... | collective-permute-start | bytes 393224 | tf_op jit(solution)/shard_map/while/body/eval_jaxpr/ppermute | solution.py:19
  87.1 6.4 %collective-permute-start = (bf16[32,2048]{1,0:T(8,128)(2,1)S(1)}, bf16[32,2048]{1,0:T(8,128)(2,1)S(1)}, u32[]{:S(2)}, u32[]{:S(2)}) collective-permute-start(bf16[32,2048]{1,0:T(8,128)(2,1)S(1)} %get-tuple-element.433), channel_id=1, source_target_pairs={{0,1},{1,2},{2,3},{3,4},{4,5},{5,6},{6,7},{7,8},{8,9},{9,10},{10,1... | collective-permute-start | bytes 393224 | tf_op jit(solution)/shard_map/while/body/eval_jaxpr/ppermute | solution.py:19
  100.6 6.2 %collective-permute-start = (bf16[32,2048]{1,0:T(8,128)(2,1)S(1)}, bf16[32,2048]{1,0:T(8,128)(2,1)S(1)}, u32[]{:S(2)}, u32[]{:S(2)}) collective-permute-start(bf16[32,2048]{1,0:T(8,128)(2,1)S(1)} %get-tuple-element.433), channel_id=1, source_target_pairs={{0,1},{1,2},{2,3},{3,4},{4,5},{5,6},{6,7},{7,8},{8,9},{9,10},{10,1... | collective-permute-start | bytes 393224 | tf_op jit(solution)/shard_map/while/body/eval_jaxpr/ppermute | solution.py:19
  114.0 6.4 %collective-permute-start = (bf16[32,2048]{1,0:T(8,128)(2,1)S(1)}, bf16[32,2048]{1,0:T(8,128)(2,1)S(1)}, u32[]{:S(2)}, u32[]{:S(2)}) collective-permute-start(bf16[32,2048]{1,0:T(8,128)(2,1)S(1)} %get-tuple-element.433), channel_id=1, source_target_pairs={{0,1},{1,2},{2,3},{3,4},{4,5},{5,6},{6,7},{7,8},{8,9},{9,10},{10,1... | collective-permute-start | bytes 393224 | tf_op jit(solution)/shard_map/while/body/eval_jaxpr/ppermute | solution.py:19
  121.1 12.7 %collective-permute-start = (bf16[32,2048]{1,0:T(8,128)(2,1)S(1)}, bf16[32,2048]{1,0:T(8,128)(2,1)S(1)}, u32[]{:S(2)}, u32[]{:S(2)}) collective-permute-start(bf16[32,2048]{1,0:T(8,128)(2,1)S(1)} %get-tuple-element.433), channel_id=1, source_target_pairs={{0,1},{1,2},{2,3},{3,4},{4,5},{5,6},{6,7},{7,8},{8,9},{9,10},{10,1... | collective-permute-start | bytes 393224 | tf_op jit(solution)/shard_map/while/body/eval_jaxpr/ppermute | solution.py:19
  134.5 6.3 %collective-permute-start = (bf16[32,2048]{1,0:T(8,128)(2,1)S(1)}, bf16[32,2048]{1,0:T(8,128)(2,1)S(1)}, u32[]{:S(2)}, u32[]{:S(2)}) collective-permute-start(bf16[32,2048]{1,0:T(8,128)(2,1)S(1)} %get-tuple-element.433), channel_id=1, source_target_pairs={{0,1},{1,2},{2,3},{3,4},{4,5},{5,6},{6,7},{7,8},{8,9},{9,10},{10,1... | collective-permute-start | bytes 393224 | tf_op jit(solution)/shard_map/while/body/eval_jaxpr/ppermute | solution.py:19
  141.5 12.8 %collective-permute-start = (bf16[32,2048]{1,0:T(8,128)(2,1)S(1)}, bf16[32,2048]{1,0:T(8,128)(2,1)S(1)}, u32[]{:S(2)}, u32[]{:S(2)}) collective-permute-start(bf16[32,2048]{1,0:T(8,128)(2,1)S(1)} %get-tuple-element.433), channel_id=1, source_target_pairs={{0,1},{1,2},{2,3},{3,4},{4,5},{5,6},{6,7},{7,8},{8,9},{9,10},{10,1... | collective-permute-start | bytes 393224 | tf_op jit(solution)/shard_map/while/body/eval_jaxpr/ppermute | solution.py:19
  155.0 6.3 %collective-permute-start = (bf16[32,2048]{1,0:T(8,128)(2,1)S(1)}, bf16[32,2048]{1,0:T(8,128)(2,1)S(1)}, u32[]{:S(2)}, u32[]{:S(2)}) collective-permute-start(bf16[32,2048]{1,0:T(8,128)(2,1)S(1)} %get-tuple-element.433), channel_id=1, source_target_pairs={{0,1},{1,2},{2,3},{3,4},{4,5},{5,6},{6,7},{7,8},{8,9},{9,10},{10,1... | collective-permute-start | bytes 393224 | tf_op jit(solution)/shard_map/while/body/eval_jaxpr/ppermute | solution.py:19
  162.0 8.2 %collective-permute-start = (bf16[32,2048]{1,0:T(8,128)(2,1)S(1)}, bf16[32,2048]{1,0:T(8,128)(2,1)S(1)}, u32[]{:S(2)}, u32[]{:S(2)}) collective-permute-start(bf16[32,2048]{1,0:T(8,128)(2,1)S(1)} %get-tuple-element.433), channel_id=1, source_target_pairs={{0,1},{1,2},{2,3},{3,4},{4,5},{5,6},{6,7},{7,8},{8,9},{9,10},{10,1... | collective-permute-start | bytes 393224 | tf_op jit(solution)/shard_map/while/body/eval_jaxpr/ppermute | solution.py:19
  170.9 7.2 %collective-permute-start = (bf16[32,2048]{1,0:T(8,128)(2,1)S(1)}, bf16[32,2048]{1,0:T(8,128)(2,1)S(1)}, u32[]{:S(2)}, u32[]{:S(2)}) collective-permute-start(bf16[32,2048]{1,0:T(8,128)(2,1)S(1)} %get-tuple-element.433), channel_id=1, source_target_pairs={{0,1},{1,2},{2,3},{3,4},{4,5},{5,6},{6,7},{7,8},{8,9},{9,10},{10,1... | collective-permute-start | bytes 393224 | tf_op jit(solution)/shard_map/while/body/eval_jaxpr/ppermute | solution.py:19
  178.8 13.7 %collective-permute-start = (bf16[32,2048]{1,0:T(8,128)(2,1)S(1)}, bf16[32,2048]{1,0:T(8,128)(2,1)S(1)}, u32[]{:S(2)}, u32[]{:S(2)}) collective-permute-start(bf16[32,2048]{1,0:T(8,128)(2,1)S(1)} %get-tuple-element.433), channel_id=1, source_target_pairs={{0,1},{1,2},{2,3},{3,4},{4,5},{5,6},{6,7},{7,8},{8,9},{9,10},{10,1... | collective-permute-start | bytes 393224 | tf_op jit(solution)/shard_map/while/body/eval_jaxpr/ppermute | solution.py:19
  193.2 7.2 %collective-permute-start = (bf16[32,2048]{1,0:T(8,128)(2,1)S(1)}, bf16[32,2048]{1,0:T(8,128)(2,1)S(1)}, u32[]{:S(2)}, u32[]{:S(2)}) collective-permute-start(bf16[32,2048]{1,0:T(8,128)(2,1)S(1)} %get-tuple-element.433), channel_id=1, source_target_pairs={{0,1},{1,2},{2,3},{3,4},{4,5},{5,6},{6,7},{7,8},{8,9},{9,10},{10,1... | collective-permute-start | bytes 393224 | tf_op jit(solution)/shard_map/while/body/eval_jaxpr/ppermute | solution.py:19
  201.1 7.2 %collective-permute-start = (bf16[32,2048]{1,0:T(8,128)(2,1)S(1)}, bf16[32,2048]{1,0:T(8,128)(2,1)S(1)}, u32[]{:S(2)}, u32[]{:S(2)}) collective-permute-start(bf16[32,2048]{1,0:T(8,128)(2,1)S(1)} %get-tuple-element.433), channel_id=1, source_target_pairs={{0,1},{1,2},{2,3},{3,4},{4,5},{5,6},{6,7},{7,8},{8,9},{9,10},{10,1... | collective-permute-start | bytes 393224 | tf_op jit(solution)/shard_map/while/body/eval_jaxpr/ppermute | solution.py:19
  209.0 7.2 %collective-permute-start = (bf16[32,2048]{1,0:T(8,128)(2,1)S(1)}, bf16[32,2048]{1,0:T(8,128)(2,1)S(1)}, u32[]{:S(2)}, u32[]{:S(2)}) collective-permute-start(bf16[32,2048]{1,0:T(8,128)(2,1)S(1)} %get-tuple-element.433), channel_id=1, source_target_pairs={{0,1},{1,2},{2,3},{3,4},{4,5},{5,6},{6,7},{7,8},{8,9},{9,10},{10,1... | collective-permute-start | bytes 393224 | tf_op jit(solution)/shard_map/while/body/eval_jaxpr/ppermute | solution.py:19
  216.9 7.6 %collective-permute-start = (bf16[32,2048]{1,0:T(8,128)(2,1)S(1)}, bf16[32,2048]{1,0:T(8,128)(2,1)S(1)}, u32[]{:S(2)}, u32[]{:S(2)}) collective-permute-start(bf16[32,2048]{1,0:T(8,128)(2,1)S(1)} %get-tuple-element.433), channel_id=1, source_target_pairs={{0,1},{1,2},{2,3},{3,4},{4,5},{5,6},{6,7},{7,8},{8,9},{9,10},{10,1... | collective-permute-start | bytes 393224 | tf_op jit(solution)/shard_map/while/body/eval_jaxpr/ppermute | solution.py:19
  225.2 7.2 %collective-permute-start = (bf16[32,2048]{1,0:T(8,128)(2,1)S(1)}, bf16[32,2048]{1,0:T(8,128)(2,1)S(1)}, u32[]{:S(2)}, u32[]{:S(2)}) collective-permute-start(bf16[32,2048]{1,0:T(8,128)(2,1)S(1)} %get-tuple-element.433), channel_id=1, source_target_pairs={{0,1},{1,2},{2,3},{3,4},{4,5},{5,6},{6,7},{7,8},{8,9},{9,10},{10,1... | collective-permute-start | bytes 393224 | tf_op jit(solution)/shard_map/while/body/eval_jaxpr/ppermute | solution.py:19
  233.2 7.2 %collective-permute-start = (bf16[32,2048]{1,0:T(8,128)(2,1)S(1)}, bf16[32,2048]{1,0:T(8,128)(2,1)S(1)}, u32[]{:S(2)}, u32[]{:S(2)}) collective-permute-start(bf16[32,2048]{1,0:T(8,128)(2,1)S(1)} %get-tuple-element.433), channel_id=1, source_target_pairs={{0,1},{1,2},{2,3},{3,4},{4,5},{5,6},{6,7},{7,8},{8,9},{9,10},{10,1... | collective-permute-start | bytes 393224 | tf_op jit(solution)/shard_map/while/body/eval_jaxpr/ppermute | solution.py:19
  241.1 7.2 %collective-permute-start = (bf16[32,2048]{1,0:T(8,128)(2,1)S(1)}, bf16[32,2048]{1,0:T(8,128)(2,1)S(1)}, u32[]{:S(2)}, u32[]{:S(2)}) collective-permute-start(bf16[32,2048]{1,0:T(8,128)(2,1)S(1)} %get-tuple-element.433), channel_id=1, source_target_pairs={{0,1},{1,2},{2,3},{3,4},{4,5},{5,6},{6,7},{7,8},{8,9},{9,10},{10,1... | collective-permute-start | bytes 393224 | tf_op jit(solution)/shard_map/while/body/eval_jaxpr/ppermute | solution.py:19
  249.0 8.6 %collective-permute-start = (bf16[32,2048]{1,0:T(8,128)(2,1)S(1)}, bf16[32,2048]{1,0:T(8,128)(2,1)S(1)}, u32[]{:S(2)}, u32[]{:S(2)}) collective-permute-start(bf16[32,2048]{1,0:T(8,128)(2,1)S(1)} %get-tuple-element.433), channel_id=1, source_target_pairs={{0,1},{1,2},{2,3},{3,4},{4,5},{5,6},{6,7},{7,8},{8,9},{9,10},{10,1... | collective-permute-start | bytes 393224 | tf_op jit(solution)/shard_map/while/body/eval_jaxpr/ppermute | solution.py:19
  257.5 64.9 %copy-start = (f32[1,224,2048]{2,1,0:T(8,128)}, f32[1,224,2048]{2,1,0:T(8,128)S(1)}, u32[]{:S(2)}) copy-start(f32[1,224,2048]{2,1,0:T(8,128)S(1)} %get-tuple-element.273) | copy-start | bytes 5505028
